TPU v7x, 1024 devices: a whole 4x4x32 slice. The times are simulated.
1024 devices in a mesh: seq: 128 (over y, z), head: 8 (over x, core).
Axes of the slice: x: 4, y: 4, z: 32, core: 2. Of those that a mesh axis runs over, the one named last changes fastest.
Arguments:
- queries: bfloat16 [16384, 2048], P('seq', 'head'), may hold values from -6 to 6
- keys: bfloat16 [16384, 2048], P('seq', 'head'), may hold values from -6 to 6
- values: bfloat16 [16384, 2048], P('seq', 'head'), may hold values from -6 to 6
- grad_out: bfloat16 [16384, 2048], P('seq', 'head'), may hold values from -6 to 6
Outputs:
- grad_queries: bfloat16 [16384, 2048], P(('seq', 'head'))
- grad_keys: bfloat16 [16384, 2048], P(('seq', 'head'))
- grad_values: bfloat16 [16384, 2048], P(('seq', 'head'))
All inputs are finite; a program needn't handle non-finite values.
Results may differ from a plain program's by a relative error of at most 0.0049.
Values may be sent and summed in bfloat16 or wider, within the bound.
No kernel may reach another device: no remote copies, remote signals or barrier semaphores. Data moves between devices by JAX's collectives and lax.ppermute only.
A program may use at most 128 MiB of HBM per device.

v0:
```python
import math

import jax
import jax.numpy as jnp
from jax import lax
from jax.sharding import PartitionSpec as P

DH = 128


def prefix(value, axis, join, neutral, backward):
    count, mine = (lax.axis_size(axis), lax.axis_index(axis))
    pieces = lax.all_gather(value, axis)
    if backward:
        pieces = pieces[::-1]
        mine = count - 1 - mine
    total = jnp.full_like(value, 0) + jnp.asarray(neutral, value.dtype)

    def step(position, total):
        longer = join(total, pieces[position])
        return jnp.where(position < mine, longer, total)

    return lax.fori_loop(0, count - 1, step, total)


def add_states(earlier, later_one):
    return earlier + later_one


def on_device(queries, keys, values, grad_out):
    tokens = queries.shape[0]
    head_dim = DH
    local_heads = queries.shape[1] // head_dim
    length = tokens * lax.axis_size("seq")
    scale = 1.0 / math.sqrt(head_dim * length)
    shape3 = (tokens, local_heads, head_dim)
    q_blk = queries.reshape(shape3)
    k_blk = keys.reshape(shape3)
    v_blk = values.reshape(shape3)
    g_blk = grad_out.reshape(shape3)
    kv_local = scale * jnp.einsum("thd,the->hde", k_blk, v_blk, preferred_element_type=jnp.float32)
    qg_local = scale * jnp.einsum("thd,the->hde", q_blk, g_blk, preferred_element_type=jnp.float32)
    zeros = jnp.zeros_like(kv_local)
    state = prefix(kv_local, "seq", add_states, zeros, False)
    later = prefix(qg_local, "seq", add_states, zeros, True)
    state = state.astype(jnp.bfloat16)
    later = later.astype(jnp.bfloat16)
    rows = jnp.arange(tokens, dtype=jnp.int32)
    causal = (rows[:, None] >= rows[None, :]).astype(jnp.float32) * scale
    scores = jnp.einsum("thd,shd->hts", q_blk, k_blk, preferred_element_type=jnp.float32)
    probs = (scores * causal[None]).astype(jnp.bfloat16)
    grads = jnp.einsum("thd,shd->hts", g_blk, v_blk, preferred_element_type=jnp.float32)
    dprobs = (grads * causal[None]).astype(jnp.bfloat16)
    d_query = jnp.einsum("hts,shd->thd", dprobs, k_blk, preferred_element_type=jnp.float32)
    d_query = d_query + jnp.einsum("the,hde->thd", g_blk, state, preferred_element_type=jnp.float32)
    d_key = jnp.einsum("hts,thd->shd", dprobs, q_blk, preferred_element_type=jnp.float32)
    d_key = d_key + jnp.einsum("the,hde->thd", v_blk, later, preferred_element_type=jnp.float32)
    d_value = jnp.einsum("hts,the->she", probs, g_blk, preferred_element_type=jnp.float32)
    d_value = d_value + jnp.einsum("thd,hde->the", k_blk, later, preferred_element_type=jnp.float32)
    flat = (tokens, local_heads * head_dim)
    d_query = d_query.astype(jnp.bfloat16).reshape(flat)
    d_key = d_key.astype(jnp.bfloat16).reshape(flat)
    d_value = d_value.astype(jnp.bfloat16).reshape(flat)
    out_query, out_key, out_value = (
        lax.all_to_all(d_query, "head", split_axis=0, concat_axis=1, tiled=True),
        lax.all_to_all(d_key, "head", split_axis=0, concat_axis=1, tiled=True),
        lax.all_to_all(d_value, "head", split_axis=0, concat_axis=1, tiled=True),
    )
    return (out_query, out_key, out_value)


def solution(mesh):
    in_specs = (P("seq", "head"), P("seq", "head"), P("seq", "head"), P("seq", "head"))
    out_specs = (P(("seq", "head"), None), P(("seq", "head"), None), P(("seq", "head"), None))
    return jax.shard_map(
        on_device, mesh=mesh, in_specs=in_specs, out_specs=out_specs, check_vma=False
    )
```

profile of v0, /device:TPU:1, one launch (start us, length us, event | category | flops | bytes accessed | tf_op | source)
XLA Modules:
  0.0 781.7 jit_solution(653974240009054824)
XLA Ops:
  7.2 1.7 convolution_multiply_fusion.1
  9.1 1.7 convolution_multiply_fusion.2
  10.8 1.0 fusion.3
  11.9 1.1 convolution_bitcast_fusion.3
  13.1 1.2 convolution_bitcast_fusion.1
  14.3 297.1 %all-gather.7.cloned.1.call-done = f32[256,128,128]{2,1,0:T(8,128)} async-done(((f32[2,128,128]{2,1,0:T(8,128)}), f32[256,128,128]{2,1,0:T(8,128)}) %all-gather.7.cloned.1.call-update) | async-done | bytes 16777232 | tf_op jit(solution)/shard_map/all_gather | solution.py:13
  311.5 11.6 %rev.3 = f32[128,2,128,128]{3,2,1,0:T(8,128)} reverse(f32[128,2,128,128]{3,2,1,0:T(8,128)} %bitcast.127), dimensions={0} | reverse | bytes 33554432 | tf_op jit(solution)/shard_map/rev | solution.py:15
  323.1 123.7 %while.29 = (s32[]{:T(128)}, f32[2,128,128]{2,1,0:T(8,128)S(1)}, s32[]{:T(128)}, f32[128,2,128,128]{3,2,1,0:T(8,128)}, s32[]{:T(128)}, /*index=5*/s32[]{:T(128)}) while((s32[]{:T(128)}, f32[2,128,128]{2,1,0:T(8,128)S(1)}, s32[]{:T(128)}, f32[128,2,128,128]{3,2,1,0:T(8,128)}, s32[]{:T(128)}, /*index=5*/s32[]{:T(128)}) %tuple.66), condition=%wide.region_3.4_spmd.clone, body=%wide.region_2.3_spmd.clone.sunk | while | flops 98308 | bytes 393309 | solution.py:23
  324.1 0.9 add_select_fusion.5
  325.1 0.9 add_select_fusion.5
  326.0 0.9 add_select_fusion.5
  327.0 0.9 add_select_fusion.5
  328.0 0.9 add_select_fusion.5
  329.0 0.9 add_select_fusion.5
  329.9 0.9 add_select_fusion.5
  330.9 0.9 add_select_fusion.5
  331.9 0.9 add_select_fusion.5
  332.9 0.9 add_select_fusion.5
  333.8 0.9 add_select_fusion.5
  334.8 0.9 add_select_fusion.5
  335.8 0.9 add_select_fusion.5
  336.7 0.9 add_select_fusion.5
  337.7 0.9 add_select_fusion.5
  338.7 0.9 add_select_fusion.5
  339.7 0.9 add_select_fusion.5
  340.6 0.9 add_select_fusion.5
  341.6 0.9 add_select_fusion.5
  342.6 0.9 add_select_fusion.5
  343.6 0.9 add_select_fusion.5
  344.5 0.9 add_select_fusion.5
  345.5 0.9 add_select_fusion.5
  346.5 0.9 add_select_fusion.5
  347.5 0.9 add_select_fusion.5
  348.4 0.9 add_select_fusion.5
  356.2 1.0 add_select_fusion.5
  360.1 1.0 add_select_fusion.5
  366.0 1.0 add_select_fusion.5
  374.7 1.0 add_select_fusion.5
  379.6 1.0 add_select_fusion.5
  380.6 1.0 add_select_fusion.5
  389.3 1.0 add_select_fusion.5
  390.3 1.0 add_select_fusion.5
  391.3 1.0 add_select_fusion.5
  396.2 1.0 add_select_fusion.5
  399.1 1.0 add_select_fusion.5
  402.0 1.0 add_select_fusion.5
  404.9 1.0 add_select_fusion.5
  405.9 1.0 add_select_fusion.5
  406.9 1.0 add_select_fusion.5
  415.6 1.0 add_select_fusion.5
  421.5 1.0 add_select_fusion.5
  424.4 1.0 add_select_fusion.5
  425.4 1.0 add_select_fusion.5
  431.2 1.0 add_select_fusion.5
  433.2 1.0 add_select_fusion.5
  435.1 1.0 add_select_fusion.5
  436.1 1.0 add_select_fusion.5
  447.8 22.5 %all-to-all-start.1 = ((bf16[8,16,256]{2,1,0:T(8,128)(2,1)}), bf16[8,16,256]{2,1,0:T(8,128)(2,1)S(1)}, u32[]{:S(2)}, u32[]{:S(2)}) async-start(bf16[8,16,256]{2,1,0:T(8,128)(2,1)} %all_to_all.46), calls=%async_computation.1 | async-start | bytes 131072 | tf_op jit(solution)/shard_map/all_to_all | solution.py:66
  470.2 143.3 %all-gather.5.cloned.1.call-done = f32[256,128,128]{2,1,0:T(8,128)} async-done(((f32[2,128,128]{2,1,0:T(8,128)}), f32[256,128,128]{2,1,0:T(8,128)}) %all-gather.5.cloned.1.call-update) | async-done | bytes 16777232 | tf_op jit(solution)/shard_map/all_gather | solution.py:13
  613.5 123.6 %while.28 = (s32[]{:T(128)}, f32[2,128,128]{2,1,0:T(8,128)S(1)}, s32[]{:T(128)}, f32[128,2,128,128]{3,2,1,0:T(8,128)}, s32[]{:T(128)}, /*index=5*/s32[]{:T(128)}) while((s32[]{:T(128)}, f32[2,128,128]{2,1,0:T(8,128)S(1)}, s32[]{:T(128)}, f32[128,2,128,128]{3,2,1,0:T(8,128)}, s32[]{:T(128)}, /*index=5*/s32[]{:T(128)}) %tuple.73), condition=%wide.region_1.2_spmd.clone, body=%wide.region_0.1_spmd.clone.sunk | while | flops 98308 | bytes 393309 | solution.py:23
  738.0 22.5 %all-to-all-start.2 = ((bf16[8,16,256]{2,1,0:T(8,128)(2,1)}), bf16[8,16,256]{2,1,0:T(8,128)(2,1)S(1)}, u32[]{:S(2)}, u32[]{:S(2)}) async-start(bf16[8,16,256]{2,1,0:T(8,128)(2,1)} %all_to_all.50), calls=%async_computation.2 | async-start | bytes 131072 | tf_op jit(solution)/shard_map/all_to_all | solution.py:67
  761.4 3.9 all-to-all-done.2
  765.4 4.0 all-to-all-start
  770.7 3.6 all-to-all-done
  (232 shorter events, 199.7 us)
Async XLA Ops:
  7.2 1.9 copy-start
  7.2 304.3 %all-gather.7.cloned.1.call-start = ((), (), s32[]{:S(2)}) async-start(), calls=%async_computation.4 | async-start | bytes 16908288 | tf_op jit(solution)/shard_map/all_gather | solution.py:13
  9.0 604.6 %all-gather.5.cloned.1.call-start = ((), (), s32[]{:S(2)}) async-start(), calls=%async_computation.3 | async-start | bytes 16908288 | tf_op jit(solution)/shard_map/all_gather | solution.py:13
  311.5 135.3 %copy-start.2 = (bf16[128,256]{1,0:T(8,128)(2,1)S(1)}, bf16[128,256]{1,0:T(8,128)(2,1)}, u32[]{:S(2)}) copy-start(bf16[128,256]{1,0:T(8,128)(2,1)} %param.10) | copy-start | bytes 196612
  311.5 449.0 %copy-start.1 = (bf16[128,256]{1,0:T(8,128)(2,1)S(1)}, bf16[128,256]{1,0:T(8,128)(2,1)}, u32[]{:S(2)}) copy-start(bf16[128,256]{1,0:T(8,128)(2,1)} %param.11) | copy-start | bytes 196612
  447.8 290.3 %all-to-all-start.1 = ((bf16[8,16,256]{2,1,0:T(8,128)(2,1)}), bf16[8,16,256]{2,1,0:T(8,128)(2,1)S(1)}, u32[]{:S(2)}, u32[]{:S(2)}) async-start(bf16[8,16,256]{2,1,0:T(8,128)(2,1)} %all_to_all.46), calls=%async_computation.1 | async-start | bytes 131072 | tf_op jit(solution)/shard_map/all_to_all | solution.py:66
  738.0 27.3 %all-to-all-start.2 = ((bf16[8,16,256]{2,1,0:T(8,128)(2,1)}), bf16[8,16,256]{2,1,0:T(8,128)(2,1)S(1)}, u32[]{:S(2)}, u32[]{:S(2)}) async-start(bf16[8,16,256]{2,1,0:T(8,128)(2,1)} %all_to_all.50), calls=%async_computation.2 | async-start | bytes 131072 | tf_op jit(solution)/shard_map/all_to_all | solution.py:67
  765.4 8.9 %all-to-all-start = ((bf16[8,16,256]{2,1,0:T(8,128)(2,1)}), bf16[8,16,256]{2,1,0:T(8,128)(2,1)S(1)}, u32[]{:S(2)}, u32[]{:S(2)}) async-start(bf16[8,16,256]{2,1,0:T(8,128)(2,1)} %all_to_all.42), calls=%async_computation | async-start | bytes 131072 | tf_op jit(solution)/shard_map/all_to_all | solution.py:65
Sparse Core Ops, SparseCore 0:
  12.1 299.2 all-gather.6
  315.6 297.9 all-gather.4
where the time goes:
time: 787 us; the launch traced here: 782 us
  waiting for transfers between devices  448 us (57%)
  other arithmetic  241 us (31%)
  starting transfers between devices  49.1 us (6%)
  local copies, waits for them, and re-layouts  15.8 us (2%)
  between operations  14.2 us (2%)
    all_gather x2, waiting for transfers between devices, prefix(): pieces = lax.all_gather(value, axis)  440 us
    select_n x254, other arithmetic, step(): return jnp.where(position < mine, longer, total)  241 us
    all_to_all x1, starting transfers between devices, on_device(): lax.all_to_all(d_value, 'head', split_axis=0, concat_axis=1, tiled=True)  22.5 us
    all_to_all x1, starting transfers between devices, on_device(): lax.all_to_all(d_key, 'head', split_axis=0, concat_axis=1, tiled=True)  22.5 us
  transfers between devices with their start and end apart: 5, of which 4 were waited for; matrix products, arithmetic and copies ran while one was open for 33% of the time, Pallas kernels for 0%

commit v1 on v0

v1 whole, which is shorter than its diff:
```python
import math

import jax
import jax.numpy as jnp
import numpy as np
from jax import lax
from jax.sharding import Mesh, PartitionSpec as P

DH = 128
ROWS, QUADS, QUAD = 4, 8, 4
NEAR = ("row", "place")
BF16, F32 = jnp.bfloat16, jnp.float32


def dot(a, b, dims):
    return lax.dot_general(a, b, dims, preferred_element_type=F32)


def on_device(queries, keys, values, grad_out):
    tokens, width = queries.shape
    heads = width // DH
    shape3 = (tokens, heads, DH)
    q, k, v, g = (a.reshape(shape3) for a in (queries, keys, values, grad_out))
    length = tokens * ROWS * QUADS * QUAD
    scale = 1.0 / math.sqrt(DH * length)
    near = ROWS * QUAD
    part = DH // near

    kv = jnp.einsum("thd,the->hde", k, v, preferred_element_type=F32).astype(BF16)
    qg = jnp.einsum("thd,the->hde", q, g, preferred_element_type=F32).astype(BF16)

    pieces = jnp.stack([kv, qg]).reshape(2, heads, near, part, DH).transpose(2, 0, 1, 3, 4)
    with jax.named_scope("near_exchange"):
        pieces = lax.all_to_all(pieces, NEAR, 0, 0, tiled=True)
    pieces = pieces.reshape(ROWS, QUAD, 2, heads, part, DH).astype(F32)
    totals = pieces.sum(1).astype(BF16)
    sends = jnp.broadcast_to(totals[None], (QUADS,) + totals.shape)
    with jax.named_scope("far_exchange"):
        far = lax.all_to_all(sends, "quad", 0, 0, tiled=True)

    rows = jnp.arange(tokens, dtype=jnp.int32)
    causal = (rows[:, None] >= rows[None, :]).astype(F32) * scale
    scores = jnp.einsum("thd,shd->hts", q, k, preferred_element_type=F32)
    probs = (scores * causal[None]).astype(BF16)
    grads = jnp.einsum("thd,shd->hts", g, v, preferred_element_type=F32)
    dprobs = (grads * causal[None]).astype(BF16)
    dq = jnp.einsum("hts,shd->thd", dprobs, k, preferred_element_type=F32)
    dk = jnp.einsum("hts,thd->shd", dprobs, q, preferred_element_type=F32)
    dv = jnp.einsum("hts,the->she", probs, g, preferred_element_type=F32)

    far = far.astype(F32)
    mine = lax.axis_index("quad")
    index = jnp.arange(QUADS)
    before = (index < mine).astype(F32).reshape(QUADS, 1, 1, 1, 1)
    after = (index > mine).astype(F32).reshape(QUADS, 1, 1, 1, 1)
    kv_row = far[:, :, 0].sum(0)
    qg_row = far[:, :, 1].sum(0)
    kv_base = (far[:, :, 0] * before).sum(0)
    qg_base = (far[:, :, 1] * after).sum(0)
    outs = []
    for row in range(ROWS):
        kv_run = kv_base[row] + sum((kv_row[r] for r in range(row)), jnp.zeros_like(kv_row[0]))
        qg_run = qg_base[row] + sum((qg_row[r] for r in range(row + 1, ROWS)), jnp.zeros_like(qg_row[0]))
        kvs, qgs = [], []
        for place in range(QUAD):
            kvs.append(kv_run)
            kv_run = kv_run + pieces[row, place, 0]
        for place in reversed(range(QUAD)):
            qgs.append(qg_run)
            qg_run = qg_run + pieces[row, place, 1]
        outs += [jnp.stack([a, b]) for a, b in zip(kvs, qgs[::-1])]
    back = (jnp.stack(outs) * scale).astype(BF16)
    with jax.named_scope("near_return"):
        back = lax.all_to_all(back, NEAR, 0, 0, tiled=True)
    states = back.transpose(1, 2, 0, 3, 4).reshape(2, heads, DH, DH)
    state, later = states[0], states[1]

    dq = dq + jnp.einsum("the,hde->thd", g, state, preferred_element_type=F32)
    dk = dk + jnp.einsum("the,hde->thd", v, later, preferred_element_type=F32)
    dv = dv + jnp.einsum("thd,hde->the", k, later, preferred_element_type=F32)
    n_head = lax.axis_size(("x", "core"))
    own = tokens // n_head
    packed = jnp.stack([a.astype(BF16).reshape(n_head, own, width) for a in (dq, dk, dv)], axis=1)
    with jax.named_scope("heads_to_tokens"):
        packed = lax.all_to_all(packed, ("x", "core"), 0, 0, tiled=True)
    out = packed.transpose(1, 2, 0, 3).reshape(3, own, n_head * width)
    return out[0], out[1], out[2]


def solution(mesh):
    split = Mesh(
        np.asarray(mesh.devices).reshape(ROWS, QUADS, QUAD, 4, 2),
        ("row", "quad", "place", "x", "core"),
    )
    seq, head = ("row", "quad", "place"), ("x", "core")
    return jax.shard_map(
        on_device,
        mesh=split,
        in_specs=(P(seq, head),) * 4,
        out_specs=(P(seq + head, None),) * 3,
        check_vma=False,
    )
```

time: 787 us -> 113 us (0.14)
  waiting for transfers between devices: 448 us -> 36.8 us
  other arithmetic: 241 us -> 1.05 us
  blocking collectives: 0 us -> 29.7 us
  between operations: 14.2 us -> 1 us
  starting transfers between devices: 49.1 us -> 36.8 us
  local copies, waits for them, and re-layouts: 15.8 us -> 4.48 us
    all_gather x2 -> x0, waiting for transfers between devices: 440 us -> none  [prefix(): pieces = lax.all_gather(value, axis)]
    select_n x254 -> x0, other arithmetic: 241 us -> none  [step(): return jnp.where(position < mine, longer, total)]
    all_to_all x0 -> x2, blocking collectives: none -> 29.7 us  [the longest x1 16.2 us: on_device(): pieces = lax.all_to_all(pieces, NEAR, 0, 0, tiled=True)]
    all_to_all x3 -> x2, waiting for transfers between devices: 7.52 us -> 36.8 us  [the longest x1 31.9 us: on_device(): far = lax.all_to_all(sends, 'quad', 0, 0, tiled=True)]
    all_to_all x3 -> x2, starting transfers between devices: 49 us -> 36.8 us  [the longest x1 25.4 us: on_device(): far = lax.all_to_all(sends, 'quad', 0, 0, tiled=True)]
    rev x1 -> x0, local copies, waits for them, and re-layouts: 11.6 us -> none  [prefix(): pieces = pieces[::-1]]
  transfers between devices with their start and end apart: 5 -> 2, of which waited for: 4 -> 2; matrix products, arithmetic and copies ran while one was open for 33% -> 1% of each run, Pallas kernels for 0% -> 0%
where the time goes in v1:
time: 113 us; the launch traced here: 112 us
  starting transfers between devices  36.8 us (33%)
  waiting for transfers between devices  36.8 us (33%)
  blocking collectives  29.7 us (26%)
  local copies, waits for them, and re-layouts  4.48 us (4%)
  matrix products  2.69 us (2%)
    all_to_all x1, waiting for transfers between devices, on_device(): far = lax.all_to_all(sends, 'quad', 0, 0, tiled=True)  31.9 us
    all_to_all x1, starting transfers between devices, on_device(): far = lax.all_to_all(sends, 'quad', 0, 0, tiled=True)  25.4 us
    all_to_all x1, blocking collectives, on_device(): pieces = lax.all_to_all(pieces, NEAR, 0, 0, tiled=True)  16.2 us
    all_to_all x1, blocking collectives, on_device(): packed = lax.all_to_all(packed, ('x', 'core'), 0, 0, tiled=True)  13.5 us
    all_to_all x1, starting transfers between devices, on_device(): back = lax.all_to_all(back, NEAR, 0, 0, tiled=True)  11.4 us
    all_to_all x1, waiting for transfers between devices, on_device(): back = lax.all_to_all(back, NEAR, 0, 0, tiled=True)  4.88 us
    unnamed x11, local copies, waits for them, and re-layouts  3.36 us
  transfers between devices with their start and end apart: 2, of which 2 were waited for; matrix products, arithmetic and copies ran while one was open for 1% of the time, Pallas kernels for 0%

profile of v1, /device:TPU:1, one launch (start us, length us, event | category | flops | bytes accessed | tf_op | source)
XLA Modules:
  0.0 112.4 jit_solution(17720576017441703536)
XLA Ops:
  0.6 0.0 copy-start
  0.6 0.0 copy-start.3
  0.7 1.1 fusion.8
  1.8 0.0 copy-done
  1.8 0.0 copy-done.3
  1.8 0.2 fusion.9
  2.0 16.2 %all_to_all.20 = bf16[16,2,2,8,128]{4,3,2,1,0:T(8,128)(2,1)S(1)} all-to-all(bf16[16,2,2,8,128]{4,3,2,1,0:T(8,128)(2,1)S(1)} %copy_bitcast_fusion), channel_id=1, replica_groups=mesh['row'=4,'quad'=8,'place'=4,'x'=4,'core'=2] {'row','place'}, dimensions={0} | all-to-all | bytes 262144 | tf_op jit(solution)/shard_map/near_exchange/all_to_all | solution.py:34
  18.3 0.7 broadcast_in_dim.2
  19.0 25.4 %all-to-all-start.1 = ((bf16[8,4,2,2,8,128]{5,4,3,2,1,0:T(8,128)(2,1)}), bf16[8,4,2,2,8,128]{5,4,3,2,1,0:T(8,128)(2,1)S(1)}, u32[]{:S(2)}, u32[]{:S(2)}) async-start(bf16[8,4,2,2,8,128]{5,4,3,2,1,0:T(8,128)(2,1)} %broadcast_in_dim.2), calls=%async_computation.1 | async-start | bytes 524288 | tf_op jit(solution)/shard_map/far_exchange/all_to_all | solution.py:39
  44.4 31.9 %all-to-all-done.1 = bf16[8,4,2,2,8,128]{5,4,3,2,1,0:T(8,128)(2,1)S(1)} async-done(((bf16[8,4,2,2,8,128]{5,4,3,2,1,0:T(8,128)(2,1)}), bf16[8,4,2,2,8,128]{5,4,3,2,1,0:T(8,128)(2,1)S(1)}, u32[]{:S(2)}, u32[]{:S(2)}) %all-to-all-start.1) | async-done | bytes 262176 | tf_op jit(solution)/shard_map/far_exchange/all_to_all | solution.py:39
  76.4 0.1 fusion.11
  76.8 0.7 multiply_convert_fusion
  77.4 11.4 %all-to-all-start.2 = ((bf16[16,2,2,8,128]{4,3,2,1,0:T(8,128)(2,1)}), bf16[16,2,2,8,128]{4,3,2,1,0:T(8,128)(2,1)S(1)}, u32[]{:S(2)}, u32[]{:S(2)}) async-start(bf16[16,2,2,8,128]{4,3,2,1,0:T(8,128)(2,1)} %multiply_convert_fusion), calls=%async_computation.2 | async-start | bytes 262144 | tf_op jit(solution)/shard_map/near_return/all_to_all | solution.py:74
  88.8 0.0 copy-start.2
  88.9 0.8 copy-done.2
  89.7 0.2 fusion.3
  89.8 0.0 copy-start.1
  89.9 0.2 convolution_bitcast_fusion.3
  90.1 0.6 copy-done.1
  90.7 0.1 convolution_bitcast_fusion.5
  90.8 0.4 convolution_bitcast_fusion.1
  91.2 4.9 %all-to-all-done.2 = bf16[16,2,2,8,128]{4,3,2,1,0:T(8,128)(2,1)S(1)} async-done(((bf16[16,2,2,8,128]{4,3,2,1,0:T(8,128)(2,1)}), bf16[16,2,2,8,128]{4,3,2,1,0:T(8,128)(2,1)S(1)}, u32[]{:S(2)}, u32[]{:S(2)}) %all-to-all-start.2) | async-done | bytes 131104 | tf_op jit(solution)/shard_map/near_return/all_to_all | solution.py:74
  96.1 0.2 fusion.5
  96.3 0.1 copy.173
  96.4 0.2 fusion.4
  96.6 0.1 copy.167
  96.7 0.2 fusion.7
  96.9 0.1 copy.181
  97.0 13.5 %all_to_all.21 = bf16[8,3,16,256]{3,2,1,0:T(8,128)(2,1)S(1)} all-to-all(bf16[8,3,16,256]{3,2,1,0:T(8,128)(2,1)S(1)} %copy.182), channel_id=1, replica_groups=mesh['row'=4,'quad'=8,'place'=4,'x'=4,'core'=2] {'x','core'}, dimensions={0} | all-to-all | bytes 393216 | tf_op jit(solution)/shard_map/heads_to_tokens/all_to_all | solution.py:85
  110.5 0.6 copy.198
  111.1 0.6 copy.199
  111.8 0.6 copy.200
  (33 shorter events, 0.5 us)
Async XLA Ops:
  0.6 1.1 %copy-start = (bf16[128,256]{1,0:T(8,128)(2,1)S(1)}, bf16[128,256]{1,0:T(8,128)(2,1)}, u32[]{:S(2)}) copy-start(bf16[128,256]{1,0:T(8,128)(2,1)} %param.7) | copy-start | bytes 196612
  0.6 1.1 %copy-start.3 = (bf16[128,256]{1,0:T(8,128)(2,1)S(1)}, bf16[128,256]{1,0:T(8,128)(2,1)}, u32[]{:S(2)}) copy-start(bf16[128,256]{1,0:T(8,128)(2,1)} %param.4) | copy-start | bytes 196612
  19.0 57.3 %all-to-all-start.1 = ((bf16[8,4,2,2,8,128]{5,4,3,2,1,0:T(8,128)(2,1)}), bf16[8,4,2,2,8,128]{5,4,3,2,1,0:T(8,128)(2,1)S(1)}, u32[]{:S(2)}, u32[]{:S(2)}) async-start(bf16[8,4,2,2,8,128]{5,4,3,2,1,0:T(8,128)(2,1)} %broadcast_in_dim.2), calls=%async_computation.1 | async-start | bytes 524288 | tf_op jit(solution)/shard_map/far_exchange/all_to_all | solution.py:39
  77.4 18.6 %all-to-all-start.2 = ((bf16[16,2,2,8,128]{4,3,2,1,0:T(8,128)(2,1)}), bf16[16,2,2,8,128]{4,3,2,1,0:T(8,128)(2,1)S(1)}, u32[]{:S(2)}, u32[]{:S(2)}) async-start(bf16[16,2,2,8,128]{4,3,2,1,0:T(8,128)(2,1)} %multiply_convert_fusion), calls=%async_computation.2 | async-start | bytes 262144 | tf_op jit(solution)/shard_map/near_return/all_to_all | solution.py:74
  88.8 0.8 copy-start.2
  89.8 0.8 copy-start.1

commit v2 on v1

--- a/solution.py
+++ b/solution.py
@@ -7,13 +7,13 @@
 from jax.sharding import Mesh, PartitionSpec as P
 
 DH = 128
-ROWS, QUADS, QUAD = 4, 8, 4
+ROWS, QUADS, QUAD = 4, 4, 8
 NEAR = ("row", "place")
+ROW_ORDER = [2, 3, 0, 1]
+PLACE_ORDER = [4, 5, 6, 7, 0, 1, 2, 3]
+FAR_ORDER = [2, 3, 0, 1]
+NEAR_ORDER = [r * QUAD + p for r in ROW_ORDER for p in PLACE_ORDER]
 BF16, F32 = jnp.bfloat16, jnp.float32
-
-
-def dot(a, b, dims):
-    return lax.dot_general(a, b, dims, preferred_element_type=F32)
 
 
 def on_device(queries, keys, values, grad_out):
@@ -24,19 +24,22 @@
     length = tokens * ROWS * QUADS * QUAD
     scale = 1.0 / math.sqrt(DH * length)
     near = ROWS * QUAD
-    part = DH // near
+    part = 8
+    n_part = DH // part
+    hs = near // n_part
+    hh = heads // hs
 
     kv = jnp.einsum("thd,the->hde", k, v, preferred_element_type=F32).astype(BF16)
     qg = jnp.einsum("thd,the->hde", q, g, preferred_element_type=F32).astype(BF16)
-
-    pieces = jnp.stack([kv, qg]).reshape(2, heads, near, part, DH).transpose(2, 0, 1, 3, 4)
+    pieces = jnp.stack([kv, qg]).reshape(2, hs, hh, n_part, part, DH)
+    pieces = pieces.transpose(1, 3, 0, 2, 4, 5).reshape(near, 2, hh, part, DH)
     with jax.named_scope("near_exchange"):
-        pieces = lax.all_to_all(pieces, NEAR, 0, 0, tiled=True)
-    pieces = pieces.reshape(ROWS, QUAD, 2, heads, part, DH).astype(F32)
+        pieces = lax.all_to_all(pieces, NEAR, 0, 0, tiled=True, axis_index_groups=[NEAR_ORDER])
+    pieces = pieces.reshape(ROWS, QUAD, 2, hh, part, DH)
+    pieces = pieces.astype(F32)
     totals = pieces.sum(1).astype(BF16)
-    sends = jnp.broadcast_to(totals[None], (QUADS,) + totals.shape)
     with jax.named_scope("far_exchange"):
-        far = lax.all_to_all(sends, "quad", 0, 0, tiled=True)
+        far = lax.all_to_all(jnp.broadcast_to(totals[None], (QUADS,) + totals.shape), "quad", 0, 0, tiled=True, axis_index_groups=[FAR_ORDER])
 
     rows = jnp.arange(tokens, dtype=jnp.int32)
     causal = (rows[:, None] >= rows[None, :]).astype(F32) * scale
@@ -47,32 +50,35 @@
     dq = jnp.einsum("hts,shd->thd", dprobs, k, preferred_element_type=F32)
     dk = jnp.einsum("hts,thd->shd", dprobs, q, preferred_element_type=F32)
     dv = jnp.einsum("hts,the->she", probs, g, preferred_element_type=F32)
+    far, dq, dk, dv = lax.optimization_barrier((far, dq, dk, dv))
 
     far = far.astype(F32)
     mine = lax.axis_index("quad")
-    index = jnp.arange(QUADS)
+    index = jnp.array(FAR_ORDER)
     before = (index < mine).astype(F32).reshape(QUADS, 1, 1, 1, 1)
     after = (index > mine).astype(F32).reshape(QUADS, 1, 1, 1, 1)
     kv_row = far[:, :, 0].sum(0)
     qg_row = far[:, :, 1].sum(0)
     kv_base = (far[:, :, 0] * before).sum(0)
     qg_base = (far[:, :, 1] * after).sum(0)
-    outs = []
-    for row in range(ROWS):
-        kv_run = kv_base[row] + sum((kv_row[r] for r in range(row)), jnp.zeros_like(kv_row[0]))
-        qg_run = qg_base[row] + sum((qg_row[r] for r in range(row + 1, ROWS)), jnp.zeros_like(qg_row[0]))
-        kvs, qgs = [], []
+    zero = jnp.zeros_like(kv_row[0])
+    outs = {}
+    for i, row in enumerate(ROW_ORDER):
+        kv_run = kv_base[i] + sum((kv_row[j] for j, r in enumerate(ROW_ORDER) if r < row), zero)
+        qg_run = qg_base[i] + sum((qg_row[j] for j, r in enumerate(ROW_ORDER) if r > row), zero)
+        kvs, qgs = {}, {}
         for place in range(QUAD):
-            kvs.append(kv_run)
-            kv_run = kv_run + pieces[row, place, 0]
+            kvs[place] = kv_run
+            kv_run = kv_run + pieces[i, PLACE_ORDER.index(place), 0]
         for place in reversed(range(QUAD)):
-            qgs.append(qg_run)
-            qg_run = qg_run + pieces[row, place, 1]
-        outs += [jnp.stack([a, b]) for a, b in zip(kvs, qgs[::-1])]
-    back = (jnp.stack(outs) * scale).astype(BF16)
+            qgs[place] = qg_run
+            qg_run = qg_run + pieces[i, PLACE_ORDER.index(place), 1]
+        for j, place in enumerate(PLACE_ORDER):
+            outs[i * QUAD + j] = jnp.stack([kvs[place], qgs[place]])
+    back = (jnp.stack([outs[i] for i in range(near)]) * scale).astype(BF16)
     with jax.named_scope("near_return"):
-        back = lax.all_to_all(back, NEAR, 0, 0, tiled=True)
-    states = back.transpose(1, 2, 0, 3, 4).reshape(2, heads, DH, DH)
+        back = lax.all_to_all(back, NEAR, 0, 0, tiled=True, axis_index_groups=[NEAR_ORDER])
+    states = back.reshape(hs, n_part, 2, hh, part, DH).transpose(2, 0, 3, 1, 4, 5).reshape(2, heads, DH, DH)
     state, later = states[0], states[1]
 
     dq = dq + jnp.einsum("the,hde->thd", g, state, preferred_element_type=F32)

time: 113 us -> 89.2 us (0.79)
  waiting for transfers between devices: 36.8 us -> 4.14 us
  starting transfers between devices: 36.8 us -> 43.1 us
  blocking collectives: 29.7 us -> 32.1 us
    all_to_all x2, waiting for transfers between devices: 36.8 us -> 4.14 us  [the longest x1 2.54 us: on_device(): lax.all_to_all(pieces, NEAR, 0, 0, tiled=True, axis_index_groups=[NEAR_OR...]
    all_to_all x2, starting transfers between devices: 36.8 us -> 43.1 us  [the longest x1 26.2 us: on_device(): lax.all_to_all(jnp.broadcast_to(totals[None], (QUADS,) + totals.shape), '...]
    all_to_all x1, blocking collectives: 13.5 us -> 15.9 us  [on_device(): packed = lax.all_to_all(packed, ('x', 'core'), 0, 0, tiled=True)]
    unnamed x11 -> x13, local copies, waits for them, and re-layouts: 3.36 us -> 3.4 us
where the time goes in v2:
time: 89.2 us; the launch traced here: 88.8 us
  starting transfers between devices  43.1 us (48%)
  blocking collectives  32.1 us (36%)
  local copies, waits for them, and re-layouts  5.13 us (6%)
  waiting for transfers between devices  4.14 us (5%)
  matrix products  2.72 us (3%)
  between operations  1.12 us (1%)
    all_to_all x1, starting transfers between devices, on_device(): lax.all_to_all(jnp.broadcast_to(totals[None], (QUADS,) + totals.shape), '...  26.2 us
    all_to_all x1, starting transfers between devices, on_device(): lax.all_to_all(pieces, NEAR, 0, 0, tiled=True, axis_index_groups=[NEAR_OR...  16.9 us
    all_to_all x1, blocking collectives, on_device(): lax.all_to_all(back, NEAR, 0, 0, tiled=True, axis_index_groups=[NEAR_ORDER])  16.3 us
    all_to_all x1, blocking collectives, on_device(): packed = lax.all_to_all(packed, ('x', 'core'), 0, 0, tiled=True)  15.9 us
    unnamed x13, local copies, waits for them, and re-layouts  3.4 us
    all_to_all x1, waiting for transfers between devices, on_device(): lax.all_to_all(pieces, NEAR, 0, 0, tiled=True, axis_index_groups=[NEAR_OR...  2.54 us
  transfers between devices with their start and end apart: 2, of which 2 were waited for; matrix products, arithmetic and copies ran while one was open for 1% of the time, Pallas kernels for 0%

profile of v2, /device:TPU:1, one launch (start us, length us, event | category | flops | bytes accessed | tf_op | source)
XLA Modules:
  0.0 88.8 jit_solution(17791187230917242956)
XLA Ops:
  0.6 0.0 copy-start
  0.6 0.0 copy-start.2
  0.7 1.1 %fusion.9 = bf16[1,2,1,16,8,128]{5,4,3,1,2,0:T(8,128)(2,1)S(1)} fusion(bf16[128,256]{1,0:T(8,128)(2,1)} %param.8, bf16[128,256]{1,0:T(8,128)(2,1)} %param.5), kind=kOutput, calls=%fused_computation.19 | convolution fusion | flops 8421376 | bytes 196608 | tf_op jit(solution)/shard_map/thd,the->hde/dot_general | solution.py:33
  1.8 0.0 copy-done
  1.8 0.0 copy-done.2
  1.8 0.2 fusion.8
  2.0 0.7 copy.433
  2.7 16.9 %all-to-all-start = ((bf16[32,2,1,8,128]{4,3,1,2,0:T(8,128)(2,1)}), bf16[32,2,1,8,128]{4,3,1,2,0:T(8,128)(2,1)S(1)}, u32[]{:S(2)}, u32[]{:S(2)}) async-start(bf16[32,2,1,8,128]{4,3,1,2,0:T(8,128)(2,1)} %bitcast.3), calls=%async_computation | async-start | bytes 262144 | tf_op jit(solution)/shard_map/near_exchange/all_to_all | solution.py:37
  19.6 0.0 copy-start.1
  19.6 0.8 copy-done.1
  20.4 0.0 copy-start.3
  20.4 0.2 fusion.3
  20.6 0.7 copy-done.3
  21.3 0.2 convolution_bitcast_fusion.4
  21.5 0.1 convolution_bitcast_fusion.5
  21.6 2.5 %all-to-all-done = bf16[32,2,1,8,128]{4,3,1,2,0:T(8,128)(2,1)S(1)} async-done(((bf16[32,2,1,8,128]{4,3,1,2,0:T(8,128)(2,1)}), bf16[32,2,1,8,128]{4,3,1,2,0:T(8,128)(2,1)S(1)}, u32[]{:S(2)}, u32[]{:S(2)}) %all-to-all-start) | async-done | bytes 131104 | tf_op jit(solution)/shard_map/near_exchange/all_to_all | solution.py:37
  24.2 0.6 broadcast_in_dim.2
  24.9 0.0 copy-start.4
  24.9 26.2 %all-to-all-start.1 = ((bf16[4,4,2,1,8,128]{5,4,3,2,1,0:T(8,128)(2,1)}), bf16[4,4,2,1,8,128]{5,4,3,2,1,0:T(8,128)(2,1)S(1)}, u32[]{:S(2)}, u32[]{:S(2)}) async-start(bf16[4,4,2,1,8,128]{5,4,3,2,1,0:T(8,128)(2,1)} %broadcast_in_dim.2), calls=%async_computation.1 | async-start | bytes 131072 | tf_op jit(solution)/shard_map/far_exchange/all_to_all | solution.py:42
  51.1 0.0 copy-done.4
  51.1 0.4 convolution_bitcast_fusion.3
  51.5 1.6 %all-to-all-done.1 = bf16[4,4,2,1,8,128]{5,4,3,2,1,0:T(8,128)(2,1)S(1)} async-done(((bf16[4,4,2,1,8,128]{5,4,3,2,1,0:T(8,128)(2,1)}), bf16[4,4,2,1,8,128]{5,4,3,2,1,0:T(8,128)(2,1)S(1)}, u32[]{:S(2)}, u32[]{:S(2)}) %all-to-all-start.1) | async-done | bytes 65568 | tf_op jit(solution)/shard_map/far_exchange/all_to_all | solution.py:42
  53.1 0.1 fusion.27
  53.7 16.3 %all_to_all.20 = bf16[32,2,1,8,128]{4,3,1,2,0:T(8,128)(2,1)S(1)} all-to-all(bf16[32,2,1,8,128]{4,3,1,2,0:T(8,128)(2,1)S(1)} %multiply_convert_fusion), channel_id=1, replica_groups={{544,552,560,568,512,520,528,536,800,808,816,824,768,776,784,792,32,40,..., dimensions={0} | all-to-all | bytes 262144 | tf_op jit(solution)/shard_map/near_return/all_to_all | solution.py:80
  70.0 0.2 fusion.7
  70.2 0.2 fusion.6
  70.4 0.2 fusion.5
  70.5 0.1 copy.460
  70.7 0.1 copy.463
  70.8 0.1 copy.467
  71.0 15.9 %all_to_all.21 = bf16[8,3,16,256]{3,2,1,0:T(8,128)(2,1)S(1)} all-to-all(bf16[8,3,16,256]{3,2,1,0:T(8,128)(2,1)S(1)} %copy.468), channel_id=1, replica_groups=mesh['row'=4,'quad'=4,'place'=8,'x'=4,'core'=2] {'x','core'}, dimensions={0} | all-to-all | bytes 393216 | tf_op jit(solution)/shard_map/heads_to_tokens/all_to_all | solution.py:91
  86.9 0.6 copy.485
  87.5 0.6 copy.484
  88.1 0.6 copy.483
  (53 shorter events, 0.6 us)
Async XLA Ops:
  0.6 1.1 %copy-start = (bf16[128,256]{1,0:T(8,128)(2,1)S(1)}, bf16[128,256]{1,0:T(8,128)(2,1)}, u32[]{:S(2)}) copy-start(bf16[128,256]{1,0:T(8,128)(2,1)} %param.6) | copy-start | bytes 196612
  0.6 1.1 %copy-start.2 = (bf16[128,256]{1,0:T(8,128)(2,1)S(1)}, bf16[128,256]{1,0:T(8,128)(2,1)}, u32[]{:S(2)}) copy-start(bf16[128,256]{1,0:T(8,128)(2,1)} %param.7) | copy-start | bytes 196612
  2.7 21.5 %all-to-all-start = ((bf16[32,2,1,8,128]{4,3,1,2,0:T(8,128)(2,1)}), bf16[32,2,1,8,128]{4,3,1,2,0:T(8,128)(2,1)S(1)}, u32[]{:S(2)}, u32[]{:S(2)}) async-start(bf16[32,2,1,8,128]{4,3,1,2,0:T(8,128)(2,1)} %bitcast.3), calls=%async_computation | async-start | bytes 262144 | tf_op jit(solution)/shard_map/near_exchange/all_to_all | solution.py:37
  19.6 0.8 copy-start.1
  20.4 0.8 copy-start.3
  24.9 26.2 %copy-start.4 = (s32[4]{0:T(128)S(1)}, s32[4]{0:T(128)}, u32[]{:S(2)}) copy-start(s32[4]{0:T(128)} %constant.16.clone) | copy-start | bytes 52
  24.9 28.2 %all-to-all-start.1 = ((bf16[4,4,2,1,8,128]{5,4,3,2,1,0:T(8,128)(2,1)}), bf16[4,4,2,1,8,128]{5,4,3,2,1,0:T(8,128)(2,1)S(1)}, u32[]{:S(2)}, u32[]{:S(2)}) async-start(bf16[4,4,2,1,8,128]{5,4,3,2,1,0:T(8,128)(2,1)} %broadcast_in_dim.2), calls=%async_computation.1 | async-start | bytes 131072 | tf_op jit(solution)/shard_map/far_exchange/all_to_all | solution.py:42

commit v3 on v1

v3 whole, which is shorter than its diff:
```python
import functools
import math

import jax
import jax.numpy as jnp
import numpy as np
from jax import lax
from jax.experimental import pallas as pl
from jax.experimental.pallas import tpu as pltpu
from jax.sharding import Mesh, PartitionSpec as P

DH = 128
ROWS, OCTS, OCT = 4, 4, 8
NEAR = ("row", "place")
ROW_ORDER = (2, 3, 0, 1)
PLACE_ORDER = (4, 5, 6, 7, 0, 1, 2, 3)
FAR_ORDER = (2, 3, 0, 1)
NEAR_ORDER = [r * OCT + p for r in ROW_ORDER for p in PLACE_ORDER]
BF16, F32 = jnp.bfloat16, jnp.float32
VMEM = pl.BlockSpec(memory_space=pltpu.VMEM)
HBM = pl.BlockSpec(memory_space=pl.ANY)


def dot(a, b, left, right):
    return lax.dot_general(a, b, (((left,), (right,)), ((), ())), preferred_element_type=F32)


def block_kernel(scale, q_in, k_in, v_in, g_in, pieces_ref, dq_ref, dk_ref, dv_ref, k_ref, v_ref, g_ref, q_ref, sems):
    copies = [
        pltpu.make_async_copy(src, dst, sems.at[n])
        for n, (src, dst) in enumerate(((k_in, k_ref), (v_in, v_ref), (q_in, q_ref), (g_in, g_ref)))
    ]
    for copy in copies:
        copy.start()
    tokens, width = q_ref.shape
    heads, parts = width // DH, DH // 8
    seen = lax.broadcasted_iota(jnp.int32, (tokens, tokens), 0) >= lax.broadcasted_iota(
        jnp.int32, (tokens, tokens), 1
    )
    copies[0].wait()
    copies[1].wait()
    for h in range(heads):
        cols = pl.ds(h * DH, DH)
        kv = dot(k_ref[:, cols], v_ref[:, cols], 0, 0)
        pieces_ref[h * parts : (h + 1) * parts, 0] = kv.reshape(parts, 8, DH).astype(BF16)
    copies[2].wait()
    copies[3].wait()
    for h in range(heads):
        cols = pl.ds(h * DH, DH)
        q, k, v, g = q_ref[:, cols], k_ref[:, cols], v_ref[:, cols], g_ref[:, cols]
        qg = dot(q, g, 0, 0)
        pieces_ref[h * parts : (h + 1) * parts, 1] = qg.reshape(parts, 8, DH).astype(BF16)
        probs = jnp.where(seen, dot(q, k, 1, 1) * scale, 0.0).astype(BF16)
        dprobs = jnp.where(seen, dot(g, v, 1, 1) * scale, 0.0).astype(BF16)
        dq_ref[:, cols] = dot(dprobs, k, 1, 0)
        dk_ref[:, cols] = dot(dprobs, q, 0, 0)
        dv_ref[:, cols] = dot(probs, g, 0, 0)


def totals_kernel(pieces_ref, sends_ref):
    for i in range(ROWS):
        for half in range(2):
            total = jnp.sum(pieces_ref[i * OCT : (i + 1) * OCT, half].astype(F32), axis=0).astype(BF16)
            for z in range(OCTS):
                sends_ref[z, i, half] = total


def prefix_kernel(scale, far_ref, pieces_ref, back_ref):
    mine = lax.axis_index("oct")
    kv_row, qg_row, kv_base, qg_base = [], [], [], []
    for i in range(ROWS):
        kv_all, qg_all, kv_some, qg_some = 0.0, 0.0, 0.0, 0.0
        for s, z in enumerate(FAR_ORDER):
            kv = far_ref[s, i, 0].astype(F32)
            qg = far_ref[s, i, 1].astype(F32)
            kv_all, qg_all = kv_all + kv, qg_all + qg
            kv_some = kv_some + jnp.where(z < mine, kv, 0.0)
            qg_some = qg_some + jnp.where(z > mine, qg, 0.0)
        kv_row.append(kv_all)
        qg_row.append(qg_all)
        kv_base.append(kv_some)
        qg_base.append(qg_some)
    for i, row in enumerate(ROW_ORDER):
        kv_run, qg_run = kv_base[i], qg_base[i]
        for j, other in enumerate(ROW_ORDER):
            if other < row:
                kv_run = kv_run + kv_row[j]
            if other > row:
                qg_run = qg_run + qg_row[j]
        for place in range(OCT):
            at = i * OCT + PLACE_ORDER.index(place)
            back_ref[at, 0] = (kv_run * scale).astype(BF16)
            kv_run = kv_run + pieces_ref[at, 0].astype(F32)
        for place in reversed(range(OCT)):
            at = i * OCT + PLACE_ORDER.index(place)
            back_ref[at, 1] = (qg_run * scale).astype(BF16)
            qg_run = qg_run + pieces_ref[at, 1].astype(F32)


def combine_kernel(back_ref, k_ref, v_ref, g_ref, dq_ref, dk_ref, dv_ref, packed_ref):
    tokens, width = k_ref.shape
    parts = DH // 8
    groups, own = packed_ref.shape[0], packed_ref.shape[1] // 3
    for h in range(width // DH):
        cols = pl.ds(h * DH, DH)
        state = back_ref[h * parts : (h + 1) * parts, 0].astype(F32).reshape(DH, DH).astype(BF16)
        later = back_ref[h * parts : (h + 1) * parts, 1].astype(F32).reshape(DH, DH).astype(BF16)
        dq = dq_ref[:, cols] + dot(g_ref[:, cols], state, 1, 1)
        dk = dk_ref[:, cols] + dot(v_ref[:, cols], later, 1, 1)
        dv = dv_ref[:, cols] + dot(k_ref[:, cols], later, 1, 0)
        for n, out in enumerate((dq, dk, dv)):
            packed_ref[:, n * own : (n + 1) * own, cols] = out.reshape(groups, own, DH).astype(BF16)


def spread_kernel(packed_ref, oq_ref, ok_ref, ov_ref, buf, sems):
    groups, rows, width = packed_ref.shape
    own = rows // 3
    copies = []
    for n, out in enumerate((oq_ref, ok_ref, ov_ref)):
        for j in range(groups):
            buf[n, :, j * width : (j + 1) * width] = packed_ref[j, n * own : (n + 1) * own, :]
        copy = pltpu.make_async_copy(buf.at[n], out, sems.at[n])
        copy.start()
        copies.append(copy)
    for copy in copies:
        copy.wait()


def inv(x):
    return pltpu.with_memory_space_constraint(x, pltpu.VMEM)


def call(kernel, ins, outs, in_specs=None, out_specs=None, **kw):
    return pl.pallas_call(
        kernel,
        out_shape=outs,
        in_specs=in_specs or [VMEM] * len(ins),
        out_specs=out_specs or jax.tree.map(lambda _: VMEM, outs),
        **kw,
    )(*ins)


def on_device(q, k, v, g):
    tokens, width = q.shape
    heads = width // DH
    length = tokens * ROWS * OCTS * OCT
    scale = 1.0 / math.sqrt(DH * length)
    near = ROWS * OCT
    shape = lambda s, t: jax.ShapeDtypeStruct(s, t)
    vshape = lambda s, t: pltpu.VMEM(s, t)

    local, bf = vshape((tokens, width), F32), vshape((tokens, width), BF16)
    pieces, dq, dk, dv, k, v, g = call(
        functools.partial(block_kernel, scale),
        (q, k, v, g),
        (vshape((near, 2, 8, DH), BF16),) + (local,) * 3 + (bf,) * 3,
        in_specs=[HBM] * 4,
        scratch_shapes=[pltpu.VMEM((tokens, width), BF16), pltpu.SemaphoreType.DMA((4,))],
    )
    with jax.named_scope("near_exchange"):
        pieces = lax.all_to_all(pieces, NEAR, 0, 0, tiled=True, axis_index_groups=[NEAR_ORDER])
    sends = call(totals_kernel, (inv(pieces),), vshape((OCTS, ROWS, 2, 8, DH), BF16))
    with jax.named_scope("far_exchange"):
        far = lax.all_to_all(sends, "oct", 0, 0, tiled=True, axis_index_groups=[FAR_ORDER])
    back = call(
        functools.partial(prefix_kernel, scale),
        (inv(far), inv(pieces)),
        vshape((near, 2, 8, DH), BF16),
    )
    with jax.named_scope("near_return"):
        back = lax.all_to_all(back, NEAR, 0, 0, tiled=True, axis_index_groups=[NEAR_ORDER])
    groups = lax.axis_size(("x", "core"))
    own = tokens // groups
    packed = call(combine_kernel, (inv(back), inv(k), inv(v), inv(g), inv(dq), inv(dk), inv(dv)), vshape((groups, 3 * own, width), BF16))
    with jax.named_scope("heads_to_tokens"):
        packed = lax.all_to_all(packed, ("x", "core"), 0, 0, tiled=True)
    out = shape((own, groups * width), BF16)
    return call(
        spread_kernel,
        (inv(packed),),
        (out,) * 3,
        out_specs=(HBM,) * 3,
        scratch_shapes=[pltpu.VMEM((3, own, groups * width), BF16), pltpu.SemaphoreType.DMA((3,))],
    )


def solution(mesh):
    split = Mesh(
        np.asarray(mesh.devices).reshape(ROWS, OCTS, OCT, 4, 2),
        ("row", "oct", "place", "x", "core"),
    )
    seq, head = ("row", "oct", "place"), ("x", "core")
    return jax.shard_map(
        on_device,
        mesh=split,
        in_specs=(P(seq, head),) * 4,
        out_specs=(P(seq + head, None),) * 3,
        check_vma=False,
    )
```

time: 113 us -> 85 us (0.75)
  blocking collectives: 29.7 us -> 81.3 us
  starting transfers between devices: 36.8 us -> 0 us
  waiting for transfers between devices: 36.8 us -> 0 us
  local copies, waits for them, and re-layouts: 4.48 us -> 0 us
  Pallas kernels: 0 us -> 2.75 us
  matrix products: 2.69 us -> 0 us
    all_to_all x1 -> x3, blocking collectives: 16.2 us -> 65.4 us  [the longest x1 27.9 us: on_device(): lax.all_to_all(sends, 'oct', 0, 0, tiled=True, axis_index_groups=[FAR_ORD...]
    all_to_all x2 -> x0, waiting for transfers between devices: 36.8 us -> none  [the longest x1 31.9 us: on_device(): far = lax.all_to_all(sends, 'quad', 0, 0, tiled=True)]
    all_to_all x2 -> x0, starting transfers between devices: 36.8 us -> none  [the longest x1 25.4 us: on_device(): far = lax.all_to_all(sends, 'quad', 0, 0, tiled=True)]
    unnamed x11 -> x0, local copies, waits for them, and re-layouts: 3.36 us -> none
    pallas_call x0 -> x5, Pallas kernels: none -> 2.75 us  [call(): pl.pallas_call(kernel, out_shape=outs, in_specs=in_specs or [VMEM] * len(...]
    dot_general x9 -> x0, matrix products: 2.69 us -> none  [the longest x1 1.11 us: on_device(): jnp.einsum('thd,the->hde', k, v, preferred_element_type=F32).astype(BF16)]
    all_to_all x1, blocking collectives: 13.5 us -> 15.9 us  [on_device(): packed = lax.all_to_all(packed, ('x', 'core'), 0, 0, tiled=True)]
  transfers between devices with their start and end apart: 2 -> 0, of which waited for: 2 -> 0; matrix products, arithmetic and copies ran while one was open for 1% -> 0% of each run, Pallas kernels for 0% -> 0%
where the time goes in v3:
time: 85 us; the launch traced here: 84.7 us
  blocking collectives  81.3 us (96%)
  Pallas kernels  2.75 us (3%)
    all_to_all x1, blocking collectives, on_device(): lax.all_to_all(sends, 'oct', 0, 0, tiled=True, axis_index_groups=[FAR_ORD...  27.9 us
    all_to_all x1, blocking collectives, on_device(): lax.all_to_all(pieces, NEAR, 0, 0, tiled=True, axis_index_groups=[NEAR_OR...  21.3 us
    all_to_all x1, blocking collectives, on_device(): lax.all_to_all(back, NEAR, 0, 0, tiled=True, axis_index_groups=[NEAR_ORDER])  16.3 us
    all_to_all x1, blocking collectives, on_device(): packed = lax.all_to_all(packed, ('x', 'core'), 0, 0, tiled=True)  15.9 us
    pallas_call x5, Pallas kernels, call(): pl.pallas_call(kernel, out_shape=outs, in_specs=in_specs or [VMEM] * len(...  2.75 us

profile of v3, /device:TPU:1, one launch (start us, length us, event | category | flops | bytes accessed | tf_op | source)
XLA Modules:
  0.0 84.7 jit_solution(14221480120754785839)
XLA Ops:
  0.6 1.7 %shard_map.67 = (bf16[32,2,8,128]{3,2,1,0:T(8,128)(2,1)S(1)}, f32[128,256]{1,0:T(8,128)S(1)}, f32[128,256]{1,0:T(8,128)S(1)}, f32[128,256]{1,0:T(8,128)S(1)}, bf...) custom-call(bf16[128,256]{1,0:T(8,128)(2,1)} %q_in.1, ...), custom_call_target="tpu_custom_call" | custom-call | tf_op jit(solution)/shard_map/pallas_call | solution.py:134
  2.4 21.3 %all_to_all.20.pieces_ref = bf16[32,2,8,128]{3,2,1,0:T(8,128)(2,1)S(1)} all-to-all(bf16[32,2,8,128]{3,2,1,0:T(8,128)(2,1)S(1)} %get-tuple-element.10), channel_id=1, replica_groups={{544,552,560,568,512,520,528,536,800,808,816,824,768,776,784,792,32,40,..., dimensions={0} | all-to-all | bytes 262144 | tf_op jit(solution)/shard_map/near_exchange/all_to_all | solution.py:161
  23.7 27.9 %all_to_all.21.far_ref = bf16[4,4,2,8,128]{4,3,2,1,0:T(8,128)(2,1)S(1)} all-to-all(bf16[4,4,2,8,128]{4,3,2,1,0:T(8,128)(2,1)S(1)} %shard_map.68), channel_id=1, replica_groups={{128,192,0,64},{129,193,1,65},{130,194,2,66},{131,195,3,67},{132,196,4,..., dimensions={0} | all-to-all | bytes 131072 | tf_op jit(solution)/shard_map/far_exchange/all_to_all | solution.py:164
  51.6 0.1 shard_map.69
  51.6 16.3 %all_to_all.22.back_ref = bf16[32,2,8,128]{3,2,1,0:T(8,128)(2,1)S(1)} all-to-all(bf16[32,2,8,128]{3,2,1,0:T(8,128)(2,1)S(1)} %shard_map.69), channel_id=1, replica_groups={{544,552,560,568,512,520,528,536,800,808,816,824,768,776,784,792,32,40,..., dimensions={0} | all-to-all | bytes 262144 | tf_op jit(solution)/shard_map/near_return/all_to_all | solution.py:171
  67.9 0.2 shard_map.70
  68.1 15.9 %all_to_all.23.packed_ref = bf16[8,48,256]{2,1,0:T(8,128)(2,1)S(1)} all-to-all(bf16[8,48,256]{2,1,0:T(8,128)(2,1)S(1)} %shard_map.70), channel_id=1, replica_groups=mesh['row'=4,'oct'=4,'place'=8,'x'=4,'core'=2] {'x','core'}, dimensions={0} | all-to-all | bytes 393216 | tf_op jit(solution)/shard_map/heads_to_tokens/all_to_all | solution.py:176
  84.0 0.7 shard_map.71
  (1 shorter events, 0.0 us)

commit v4 on v3

v4 whole, which is shorter than its diff:
```python
import functools
import math

import jax
import jax.numpy as jnp
import numpy as np
from jax import lax
from jax.experimental import pallas as pl
from jax.experimental.pallas import tpu as pltpu
from jax.sharding import Mesh, PartitionSpec as P

DH = 128
ROWS, OCTS, OCT = 4, 4, 8
NEAR = ("row", "place")
ROW_ORDER = (2, 3, 0, 1)
PLACE_ORDER = (4, 5, 6, 7, 0, 1, 2, 3)
FAR_ORDER = (2, 3, 0, 1)
LATE = 2
HEAD_ORDER = (4, 5, 6, 7, 0, 1, 2, 3)
NEAR_ORDER = [r * OCT + p for r in ROW_ORDER for p in PLACE_ORDER]
BF16, F32 = jnp.bfloat16, jnp.float32
VMEM = pl.BlockSpec(memory_space=pltpu.VMEM)
HBM = pl.BlockSpec(memory_space=pl.ANY)


def dot(a, b, left, right):
    return lax.dot_general(a, b, (((left,), (right,)), ((), ())), preferred_element_type=F32)


def local_terms(scale, q, k, v, g):
    shape = (q.shape[0], q.shape[0])
    seen = lax.broadcasted_iota(jnp.int32, shape, 0) >= lax.broadcasted_iota(jnp.int32, shape, 1)
    probs = jnp.where(seen, dot(q, k, 1, 1) * scale, 0.0).astype(BF16)
    dprobs = jnp.where(seen, dot(g, v, 1, 1) * scale, 0.0).astype(BF16)
    return dot(dprobs, k, 1, 0), dot(dprobs, q, 0, 0), dot(probs, g, 0, 0)


def block_kernel(scale, q_in, k_in, v_in, g_in, pieces_ref, *rest):
    grads, (q_ref, k_ref, v_ref, g_ref), sems = rest[:3], rest[3:7], rest[7]
    copies = [
        pltpu.make_async_copy(src, dst, sems.at[n])
        for n, (src, dst) in enumerate(((k_in, k_ref), (v_in, v_ref), (q_in, q_ref), (g_in, g_ref)))
    ]
    for copy in copies:
        copy.start()
    heads, parts = q_ref.shape[1] // DH, DH // 8
    for half, (a_ref, b_ref) in enumerate(((k_ref, v_ref), (q_ref, g_ref))):
        copies[2 * half].wait()
        copies[2 * half + 1].wait()
        for h in range(heads):
            cols = pl.ds(h * DH, DH)
            out = dot(a_ref[:, cols], b_ref[:, cols], 0, 0)
            pieces_ref[h * parts : (h + 1) * parts, half] = out.reshape(parts, 8, DH).astype(BF16)

    @pl.when(lax.axis_index("oct") < LATE)
    def _():
        for h in range(heads):
            cols = pl.ds(h * DH, DH)
            terms = local_terms(scale, q_ref[:, cols], k_ref[:, cols], v_ref[:, cols], g_ref[:, cols])
            for ref, term in zip(grads, terms):
                ref[:, cols] = term


def totals_kernel(pieces_ref, sends_ref):
    mine = lax.axis_index("oct")
    kv, qg = [None] * ROWS, [None] * ROWS
    for i, row in enumerate(ROW_ORDER):
        kv[row] = jnp.sum(pieces_ref[i * OCT : (i + 1) * OCT, 0].astype(F32), axis=0)
        qg[row] = jnp.sum(pieces_ref[i * OCT : (i + 1) * OCT, 1].astype(F32), axis=0)
    kv_up, qg_down = kv[:1], qg[-1:]
    for row in range(1, ROWS):
        kv_up.append(kv_up[-1] + kv[row])
        qg_down.insert(0, qg[ROWS - 1 - row] + qg_down[0])
    to_later = [a.astype(BF16) for a in kv_up + qg_down[1:]]
    to_earlier = [a.astype(BF16) for a in kv_up[:-1] + qg_down]
    for s, z in enumerate(FAR_ORDER):
        @pl.when(mine < z)
        def _():
            for n, a in enumerate(to_later):
                sends_ref[s, n] = a

        @pl.when(mine >= z)
        def _():
            for n, a in enumerate(to_earlier):
                sends_ref[s, n] = a


def prefix_kernel(scale, far_ref, pieces_ref, back_ref):
    mine = lax.axis_index("oct")
    kv_far, qg_far = [0.0] * ROWS, [0.0] * ROWS
    for s, z in enumerate(FAR_ORDER):
        slots = [far_ref[s, n].astype(F32) for n in range(2 * ROWS - 1)]
        earlier, later = z < mine, z > mine
        for row in range(ROWS):
            kv = jnp.where(earlier, slots[row], 0.0)
            qg = jnp.where(later, slots[ROWS - 1 + row], 0.0)
            if row > 0:
                kv = jnp.where(later, slots[row - 1], kv)
            if row < ROWS - 1:
                qg = jnp.where(earlier, slots[ROWS + row], qg)
            kv_far[row], qg_far[row] = kv_far[row] + kv, qg_far[row] + qg
    order = [ROW_ORDER.index(row) * OCT for row in range(ROWS)]
    own = 0.0
    for row in range(ROWS):
        for place in range(OCT):
            at = order[row] + PLACE_ORDER.index(place)
            back_ref[at, 0] = ((kv_far[row] + own) * scale).astype(BF16)
            own = own + pieces_ref[at, 0].astype(F32)
    own = 0.0
    for row in reversed(range(ROWS)):
        for place in reversed(range(OCT)):
            at = order[row] + PLACE_ORDER.index(place)
            back_ref[at, 1] = ((qg_far[row] + own) * scale).astype(BF16)
            own = own + pieces_ref[at, 1].astype(F32)


def combine_kernel(scale, back_ref, q_ref, k_ref, v_ref, g_ref, dq_ref, dk_ref, dv_ref, packed_ref):
    tokens, width = k_ref.shape
    parts = DH // 8
    groups, own = packed_ref.shape[0], packed_ref.shape[1] // 3

    def head(h, local):
        cols = pl.ds(h * DH, DH)
        k, v, g = k_ref[:, cols], v_ref[:, cols], g_ref[:, cols]
        state = back_ref[h * parts : (h + 1) * parts, 0].astype(F32).reshape(DH, DH).astype(BF16)
        later = back_ref[h * parts : (h + 1) * parts, 1].astype(F32).reshape(DH, DH).astype(BF16)
        far = dot(g, state, 1, 1), dot(v, later, 1, 1), dot(k, later, 1, 0)
        for n, (a, b) in enumerate(zip(local, far)):
            out = (a + b).reshape(groups, own, DH).astype(BF16)
            for i, j in enumerate(HEAD_ORDER):
                packed_ref[i, n * own : (n + 1) * own, cols] = out[j]

    late = lax.axis_index("oct") >= LATE

    @pl.when(late)
    def _():
        for h in range(width // DH):
            cols = pl.ds(h * DH, DH)
            head(h, local_terms(scale, q_ref[:, cols], k_ref[:, cols], v_ref[:, cols], g_ref[:, cols]))

    @pl.when(jnp.logical_not(late))
    def _():
        for h in range(width // DH):
            cols = pl.ds(h * DH, DH)
            head(h, (dq_ref[:, cols], dk_ref[:, cols], dv_ref[:, cols]))


def spread_kernel(packed_ref, oq_ref, ok_ref, ov_ref, buf, sems):
    groups, rows, width = packed_ref.shape
    own = rows // 3
    copies = []
    for n, out in enumerate((oq_ref, ok_ref, ov_ref)):
        for i, j in enumerate(HEAD_ORDER):
            buf[n, :, j * width : (j + 1) * width] = packed_ref[i, n * own : (n + 1) * own, :]
        copy = pltpu.make_async_copy(buf.at[n], out, sems.at[n])
        copy.start()
        copies.append(copy)
    for copy in copies:
        copy.wait()


def inv(x):
    return pltpu.with_memory_space_constraint(x, pltpu.VMEM)


def call(kernel, ins, outs, in_specs=None, out_specs=None, **kw):
    return pl.pallas_call(
        kernel,
        out_shape=outs,
        in_specs=in_specs or [VMEM] * len(ins),
        out_specs=out_specs or jax.tree.map(lambda _: VMEM, outs),
        **kw,
    )(*ins)


def on_device(q, k, v, g):
    tokens, width = q.shape
    heads = width // DH
    length = tokens * ROWS * OCTS * OCT
    scale = 1.0 / math.sqrt(DH * length)
    near = ROWS * OCT
    shape = lambda s, t: jax.ShapeDtypeStruct(s, t)
    vshape = lambda s, t: pltpu.VMEM(s, t)

    local, bf = vshape((tokens, width), F32), vshape((tokens, width), BF16)
    pieces, dq, dk, dv, q, k, v, g = call(
        functools.partial(block_kernel, scale),
        (q, k, v, g),
        (vshape((near, 2, 8, DH), BF16),) + (local,) * 3 + (bf,) * 4,
        in_specs=[HBM] * 4,
        scratch_shapes=[pltpu.SemaphoreType.DMA((4,))],
    )
    with jax.named_scope("near_exchange"):
        pieces = lax.all_to_all(pieces, NEAR, 0, 0, tiled=True, axis_index_groups=[NEAR_ORDER])
    sends = call(totals_kernel, (inv(pieces),), vshape((OCTS, 2 * ROWS - 1, 8, DH), BF16))
    with jax.named_scope("far_exchange"):
        far = lax.all_to_all(sends, "oct", 0, 0, tiled=True, axis_index_groups=[FAR_ORDER])
    back = call(
        functools.partial(prefix_kernel, scale),
        (inv(far), inv(pieces)),
        vshape((near, 2, 8, DH), BF16),
    )
    with jax.named_scope("near_return"):
        back = lax.all_to_all(back, NEAR, 0, 0, tiled=True, axis_index_groups=[NEAR_ORDER])
    groups = lax.axis_size(("x", "core"))
    own = tokens // groups
    packed = call(functools.partial(combine_kernel, scale), tuple(map(inv, (back, q, k, v, g, dq, dk, dv))), vshape((groups, 3 * own, width), BF16))
    with jax.named_scope("heads_to_tokens"):
        packed = lax.all_to_all(packed, ("x", "core"), 0, 0, tiled=True, axis_index_groups=[HEAD_ORDER])
    out = shape((own, groups * width), BF16)
    return call(
        spread_kernel,
        (inv(packed),),
        (out,) * 3,
        out_specs=(HBM,) * 3,
        scratch_shapes=[pltpu.VMEM((3, own, groups * width), BF16), pltpu.SemaphoreType.DMA((3,))],
    )


def solution(mesh):
    split = Mesh(
        np.asarray(mesh.devices).reshape(ROWS, OCTS, OCT, 4, 2),
        ("row", "oct", "place", "x", "core"),
    )
    seq, head = ("row", "oct", "place"), ("x", "core")
    return jax.shard_map(
        on_device,
        mesh=split,
        in_specs=(P(seq, head),) * 4,
        out_specs=(P(seq + head, None),) * 3,
        check_vma=False,
    )
```

time: 85 us -> 82.8 us (0.974)
  blocking collectives: 81.3 us -> 78.9 us
    all_to_all x1, blocking collectives: 15.9 us -> 14.3 us  [on_device(): lax.all_to_all(packed, ('x', 'core'), 0, 0, tiled=True, axis_index_groups...]
where the time goes in v4:
time: 82.8 us; the launch traced here: 82.5 us
  blocking collectives  78.9 us (95%)
  Pallas kernels  2.92 us (4%)
    all_to_all x1, blocking collectives, on_device(): lax.all_to_all(sends, 'oct', 0, 0, tiled=True, axis_index_groups=[FAR_ORD...  27.3 us
    all_to_all x1, blocking collectives, on_device(): lax.all_to_all(pieces, NEAR, 0, 0, tiled=True, axis_index_groups=[NEAR_OR...  21.3 us
    all_to_all x1, blocking collectives, on_device(): lax.all_to_all(back, NEAR, 0, 0, tiled=True, axis_index_groups=[NEAR_ORDER])  16.1 us
    all_to_all x1, blocking collectives, on_device(): lax.all_to_all(packed, ('x', 'core'), 0, 0, tiled=True, axis_index_groups...  14.3 us
    pallas_call x5, Pallas kernels, call(): pl.pallas_call(kernel, out_shape=outs, in_specs=in_specs or [VMEM] * len(...  2.92 us

profile of v4, /device:TPU:1, one launch (start us, length us, event | category | flops | bytes accessed | tf_op | source)
XLA Modules:
  0.0 82.5 jit_solution(2755497699280026997)
XLA Ops:
  0.6 1.9 %shard_map.67 = (bf16[32,2,8,128]{3,2,1,0:T(8,128)(2,1)S(1)}, f32[128,256]{1,0:T(8,128)S(1)}, f32[128,256]{1,0:T(8,128)S(1)}, f32[128,256]{1,0:T(8,128)S(1)}, bf...) custom-call(bf16[128,256]{1,0:T(8,128)(2,1)} %q_in.1, ...), custom_call_target="tpu_custom_call" | custom-call | tf_op jit(solution)/shard_map/pallas_call | solution.py:167
  2.5 21.3 %all_to_all.20.pieces_ref = bf16[32,2,8,128]{3,2,1,0:T(8,128)(2,1)S(1)} all-to-all(bf16[32,2,8,128]{3,2,1,0:T(8,128)(2,1)S(1)} %get-tuple-element.11), channel_id=1, replica_groups={{544,552,560,568,512,520,528,536,800,808,816,824,768,776,784,792,32,40,..., dimensions={0} | all-to-all | bytes 262144 | tf_op jit(solution)/shard_map/near_exchange/all_to_all | solution.py:194
  23.8 27.3 %all_to_all.21.far_ref = bf16[4,7,8,128]{3,2,1,0:T(8,128)(2,1)S(1)} all-to-all(bf16[4,7,8,128]{3,2,1,0:T(8,128)(2,1)S(1)} %shard_map.68), channel_id=1, replica_groups={{128,192,0,64},{129,193,1,65},{130,194,2,66},{131,195,3,67},{132,196,4,..., dimensions={0} | all-to-all | bytes 114688 | tf_op jit(solution)/shard_map/far_exchange/all_to_all | solution.py:197
  51.1 0.1 shard_map.69
  51.2 16.1 %all_to_all.22.back_ref = bf16[32,2,8,128]{3,2,1,0:T(8,128)(2,1)S(1)} all-to-all(bf16[32,2,8,128]{3,2,1,0:T(8,128)(2,1)S(1)} %shard_map.69), channel_id=1, replica_groups={{544,552,560,568,512,520,528,536,800,808,816,824,768,776,784,792,32,40,..., dimensions={0} | all-to-all | bytes 262144 | tf_op jit(solution)/shard_map/near_return/all_to_all | solution.py:204
  67.2 0.2 shard_map.70
  67.5 14.3 %all_to_all.23.packed_ref = bf16[8,48,256]{2,1,0:T(8,128)(2,1)S(1)} all-to-all(bf16[8,48,256]{2,1,0:T(8,128)(2,1)S(1)} %shard_map.70), channel_id=1, replica_groups={{4,5,6,7,0,1,2,3},{12,13,14,15,8,9,10,11},{20,21,22,23,16,17,18,19},{28..., dimensions={0} | all-to-all | bytes 393216 | tf_op jit(solution)/shard_map/heads_to_tokens/all_to_all | solution.py:209
  81.8 0.7 shard_map.71
  (1 shorter events, 0.0 us)

commit v5 on v4

--- a/solution.py
+++ b/solution.py
@@ -13,10 +13,10 @@
 ROWS, OCTS, OCT = 4, 4, 8
 NEAR = ("row", "place")
 ROW_ORDER = (2, 3, 0, 1)
-PLACE_ORDER = (4, 5, 6, 7, 0, 1, 2, 3)
-FAR_ORDER = (2, 3, 0, 1)
+PLACE_ORDER = (4, 3, 5, 2, 6, 1, 7, 0)
+FAR_ORDER = (2, 0, 3, 1)
 LATE = 2
-HEAD_ORDER = (4, 5, 6, 7, 0, 1, 2, 3)
+HEAD_ORDER = (4, 5, 2, 3, 0, 1, 6, 7)
 NEAR_ORDER = [r * OCT + p for r in ROW_ORDER for p in PLACE_ORDER]
 BF16, F32 = jnp.bfloat16, jnp.float32
 VMEM = pl.BlockSpec(memory_space=pltpu.VMEM)

time: 82.8 us -> 82.2 us (level)
    all_to_all x1, blocking collectives: 16.1 us -> 15.1 us  [on_device(): lax.all_to_all(back, NEAR, 0, 0, tiled=True, axis_index_groups=[NEAR_ORDER])]
where the time goes in v5:
time: 82.2 us; the launch traced here: 81.9 us
  blocking collectives  78.3 us (95%)
  Pallas kernels  2.92 us (4%)
    all_to_all x1, blocking collectives, on_device(): lax.all_to_all(sends, 'oct', 0, 0, tiled=True, axis_index_groups=[FAR_ORD...  27.7 us
    all_to_all x1, blocking collectives, on_device(): lax.all_to_all(pieces, NEAR, 0, 0, tiled=True, axis_index_groups=[NEAR_OR...  21.2 us
    all_to_all x1, blocking collectives, on_device(): lax.all_to_all(back, NEAR, 0, 0, tiled=True, axis_index_groups=[NEAR_ORDER])  15.1 us
    all_to_all x1, blocking collectives, on_device(): lax.all_to_all(packed, ('x', 'core'), 0, 0, tiled=True, axis_index_groups...  14.4 us
    pallas_call x5, Pallas kernels, call(): pl.pallas_call(kernel, out_shape=outs, in_specs=in_specs or [VMEM] * len(...  2.92 us

profile of v5, /device:TPU:1, one launch (start us, length us, event | category | flops | bytes accessed | tf_op | source)
XLA Modules:
  0.0 81.9 jit_solution(14814287720339965154)
XLA Ops:
  0.6 1.9 %shard_map.67 = (bf16[32,2,8,128]{3,2,1,0:T(8,128)(2,1)S(1)}, f32[128,256]{1,0:T(8,128)S(1)}, f32[128,256]{1,0:T(8,128)S(1)}, f32[128,256]{1,0:T(8,128)S(1)}, bf...) custom-call(bf16[128,256]{1,0:T(8,128)(2,1)} %q_in.1, ...), custom_call_target="tpu_custom_call" | custom-call | tf_op jit(solution)/shard_map/pallas_call | solution.py:167
  2.5 21.2 %all_to_all.20.pieces_ref = bf16[32,2,8,128]{3,2,1,0:T(8,128)(2,1)S(1)} all-to-all(bf16[32,2,8,128]{3,2,1,0:T(8,128)(2,1)S(1)} %get-tuple-element.11), channel_id=1, replica_groups={{544,536,552,528,560,520,568,512,800,792,808,784,816,776,824,768,32,24,..., dimensions={0} | all-to-all | bytes 262144 | tf_op jit(solution)/shard_map/near_exchange/all_to_all | solution.py:194
  23.8 27.7 %all_to_all.21.far_ref = bf16[4,7,8,128]{3,2,1,0:T(8,128)(2,1)S(1)} all-to-all(bf16[4,7,8,128]{3,2,1,0:T(8,128)(2,1)S(1)} %shard_map.68), channel_id=1, replica_groups={{128,0,192,64},{129,1,193,65},{130,2,194,66},{131,3,195,67},{132,4,196,..., dimensions={0} | all-to-all | bytes 114688 | tf_op jit(solution)/shard_map/far_exchange/all_to_all | solution.py:197
  51.4 0.1 shard_map.69
  51.5 15.1 %all_to_all.22.back_ref = bf16[32,2,8,128]{3,2,1,0:T(8,128)(2,1)S(1)} all-to-all(bf16[32,2,8,128]{3,2,1,0:T(8,128)(2,1)S(1)} %shard_map.69), channel_id=1, replica_groups={{544,536,552,528,560,520,568,512,800,792,808,784,816,776,824,768,32,24,..., dimensions={0} | all-to-all | bytes 262144 | tf_op jit(solution)/shard_map/near_return/all_to_all | solution.py:204
  66.6 0.2 shard_map.70
  66.8 14.4 %all_to_all.23.packed_ref = bf16[8,48,256]{2,1,0:T(8,128)(2,1)S(1)} all-to-all(bf16[8,48,256]{2,1,0:T(8,128)(2,1)S(1)} %shard_map.70), channel_id=1, replica_groups={{4,5,2,3,0,1,6,7},{12,13,10,11,8,9,14,15},{20,21,18,19,16,17,22,23},{28..., dimensions={0} | all-to-all | bytes 393216 | tf_op jit(solution)/shard_map/heads_to_tokens/all_to_all | solution.py:209
  81.2 0.7 shard_map.71
  (1 shorter events, 0.0 us)

commit v6 on v5

--- a/solution.py
+++ b/solution.py
@@ -18,6 +18,9 @@
 LATE = 2
 HEAD_ORDER = (4, 5, 2, 3, 0, 1, 6, 7)
 NEAR_ORDER = [r * OCT + p for r in ROW_ORDER for p in PLACE_ORDER]
+RETURN_PLACES = (5, 4, 6, 3, 7, 2, 1, 0)
+RETURN_ORDER = [r * OCT + p for r in ROW_ORDER for p in RETURN_PLACES]
+SLICE_AT = [RETURN_ORDER.index(d) for d in NEAR_ORDER]
 BF16, F32 = jnp.bfloat16, jnp.float32
 VMEM = pl.BlockSpec(memory_space=pltpu.VMEM)
 HBM = pl.BlockSpec(memory_space=pl.ANY)
@@ -104,13 +107,13 @@
     for row in range(ROWS):
         for place in range(OCT):
             at = order[row] + PLACE_ORDER.index(place)
-            back_ref[at, 0] = ((kv_far[row] + own) * scale).astype(BF16)
+            back_ref[order[row] + RETURN_PLACES.index(place), 0] = ((kv_far[row] + own) * scale).astype(BF16)
             own = own + pieces_ref[at, 0].astype(F32)
     own = 0.0
     for row in reversed(range(ROWS)):
         for place in reversed(range(OCT)):
             at = order[row] + PLACE_ORDER.index(place)
-            back_ref[at, 1] = ((qg_far[row] + own) * scale).astype(BF16)
+            back_ref[order[row] + RETURN_PLACES.index(place), 1] = ((qg_far[row] + own) * scale).astype(BF16)
             own = own + pieces_ref[at, 1].astype(F32)
 
 
@@ -122,8 +125,10 @@
     def head(h, local):
         cols = pl.ds(h * DH, DH)
         k, v, g = k_ref[:, cols], v_ref[:, cols], g_ref[:, cols]
-        state = back_ref[h * parts : (h + 1) * parts, 0].astype(F32).reshape(DH, DH).astype(BF16)
-        later = back_ref[h * parts : (h + 1) * parts, 1].astype(F32).reshape(DH, DH).astype(BF16)
+        state, later = (
+            jnp.concatenate([back_ref[at, half].astype(F32) for at in SLICE_AT[h * parts : (h + 1) * parts]]).astype(BF16)
+            for half in range(2)
+        )
         far = dot(g, state, 1, 1), dot(v, later, 1, 1), dot(k, later, 1, 0)
         for n, (a, b) in enumerate(zip(local, far)):
             out = (a + b).reshape(groups, own, DH).astype(BF16)
@@ -201,7 +206,7 @@
         vshape((near, 2, 8, DH), BF16),
     )
     with jax.named_scope("near_return"):
-        back = lax.all_to_all(back, NEAR, 0, 0, tiled=True, axis_index_groups=[NEAR_ORDER])
+        back = lax.all_to_all(back, NEAR, 0, 0, tiled=True, axis_index_groups=[RETURN_ORDER])
     groups = lax.axis_size(("x", "core"))
     own = tokens // groups
     packed = call(functools.partial(combine_kernel, scale), tuple(map(inv, (back, q, k, v, g, dq, dk, dv))), vshape((groups, 3 * own, width), BF16))

time: 82.2 us -> 82.9 us (level)
    all_to_all x1, blocking collectives: 14.4 us -> 15.2 us  [on_device(): lax.all_to_all(packed, ('x', 'core'), 0, 0, tiled=True, axis_index_groups...]
where the time goes in v6:
time: 82.9 us; the launch traced here: 82.6 us
  blocking collectives  79.1 us (95%)
  Pallas kernels  2.92 us (4%)
    all_to_all x1, blocking collectives, on_device(): lax.all_to_all(sends, 'oct', 0, 0, tiled=True, axis_index_groups=[FAR_ORD...  27.7 us
    all_to_all x1, blocking collectives, on_device(): lax.all_to_all(pieces, NEAR, 0, 0, tiled=True, axis_index_groups=[NEAR_OR...  21.2 us
    all_to_all x1, blocking collectives, on_device(): lax.all_to_all(packed, ('x', 'core'), 0, 0, tiled=True, axis_index_groups...  15.2 us
    all_to_all x1, blocking collectives, on_device(): lax.all_to_all(back, NEAR, 0, 0, tiled=True, axis_index_groups=[RETURN_OR...  14.9 us
    pallas_call x5, Pallas kernels, call(): pl.pallas_call(kernel, out_shape=outs, in_specs=in_specs or [VMEM] * len(...  2.92 us

profile of v6, /device:TPU:1, one launch (start us, length us, event | category | flops | bytes accessed | tf_op | source)
XLA Modules:
  0.0 82.6 jit_solution(9526985330772918945)
XLA Ops:
  0.6 1.9 %shard_map.67 = (bf16[32,2,8,128]{3,2,1,0:T(8,128)(2,1)S(1)}, f32[128,256]{1,0:T(8,128)S(1)}, f32[128,256]{1,0:T(8,128)S(1)}, f32[128,256]{1,0:T(8,128)S(1)}, bf...) custom-call(bf16[128,256]{1,0:T(8,128)(2,1)} %q_in.1, ...), custom_call_target="tpu_custom_call" | custom-call | tf_op jit(solution)/shard_map/pallas_call | solution.py:172
  2.5 21.2 %all_to_all.20.pieces_ref = bf16[32,2,8,128]{3,2,1,0:T(8,128)(2,1)S(1)} all-to-all(bf16[32,2,8,128]{3,2,1,0:T(8,128)(2,1)S(1)} %get-tuple-element.11), channel_id=1, replica_groups={{544,536,552,528,560,520,568,512,800,792,808,784,816,776,824,768,32,24,..., dimensions={0} | all-to-all | bytes 262144 | tf_op jit(solution)/shard_map/near_exchange/all_to_all | solution.py:199
  23.8 27.7 %all_to_all.21.far_ref = bf16[4,7,8,128]{3,2,1,0:T(8,128)(2,1)S(1)} all-to-all(bf16[4,7,8,128]{3,2,1,0:T(8,128)(2,1)S(1)} %shard_map.68), channel_id=1, replica_groups={{128,0,192,64},{129,1,193,65},{130,2,194,66},{131,3,195,67},{132,4,196,..., dimensions={0} | all-to-all | bytes 114688 | tf_op jit(solution)/shard_map/far_exchange/all_to_all | solution.py:202
  51.4 0.1 shard_map.69
  51.5 14.9 %all_to_all.22.back_ref = bf16[32,2,8,128]{3,2,1,0:T(8,128)(2,1)S(1)} all-to-all(bf16[32,2,8,128]{3,2,1,0:T(8,128)(2,1)S(1)} %shard_map.69), channel_id=1, replica_groups={{552,544,560,536,568,528,520,512,808,800,816,792,824,784,776,768,40,32,..., dimensions={0} | all-to-all | bytes 262144 | tf_op jit(solution)/shard_map/near_return/all_to_all | solution.py:209
  66.4 0.2 shard_map.70
  66.7 15.2 %all_to_all.23.packed_ref = bf16[8,48,256]{2,1,0:T(8,128)(2,1)S(1)} all-to-all(bf16[8,48,256]{2,1,0:T(8,128)(2,1)S(1)} %shard_map.70), channel_id=1, replica_groups={{4,5,2,3,0,1,6,7},{12,13,10,11,8,9,14,15},{20,21,18,19,16,17,22,23},{28..., dimensions={0} | all-to-all | bytes 393216 | tf_op jit(solution)/shard_map/heads_to_tokens/all_to_all | solution.py:214
  81.9 0.7 shard_map.71
  (1 shorter events, 0.0 us)
